TPU v7x, 128 devices: a whole 4x4x4 slice. The times are simulated.
128 devices in a mesh: seq: 8 (over x, core), exp: 16 (over y, z).
Axes of the slice: x: 4, y: 4, z: 4, core: 2. Of those that a mesh axis runs over, the one named last changes fastest.
Arguments:
- xin: bfloat16 [512, 4, 8192], P('seq', None, 'exp'), may hold values from -6 to 6
- zin: bfloat16 [512, 4, 8192], P('seq', None, 'exp'), may hold values from -6 to 6
- conv_weight: float32 [4, 8192], P(None, 'exp'), may hold values from -3 to 3
- conv_bias: float32 [8192], P('exp'), may hold values from -3 to 3
- xproj_weight: bfloat16 [8192, 288], P('exp'), may hold values from -0.0625 to 0.0625
- dtproj_weight: bfloat16 [256, 8192], P(None, 'exp'), may hold values from -0.375 to 0.375
- dt_bias: float32 [8192], P('exp'), may hold values from -5 to -3
- a_log: float32 [16, 8192], P(None, 'exp'), may hold values from -3 to 1
- skip: float32 [8192], P('exp'), may hold values from 0.2 to 1
- out_weight: bfloat16 [8192, 4096], P('exp'), may hold values from -0.0625 to 0.0625
- resid: bfloat16 [512, 4, 4096], P(('seq', 'exp')), may hold values from -6 to 6
- norm_gain: float32 [4096], replicated, may hold values from 0.5 to 1.5
- expert_ids: int32 [512, 4, 2], P(('seq', 'exp')), may hold values from 0 to 7, all different within a row; in each aligned block of 16 rows (0 to 15, 16 to 31, ..., all dimensions but the last counted through in order) at most 8 rows name the same one
- gate_weights: bfloat16 [512, 4, 2], P(('seq', 'exp')), may hold values from 0.19921875 to 1
- w_gate: bfloat16 [16, 4096, 6144], P('exp', None, 'seq'), may hold values from -0.09375 to 0.09375
- w_up: bfloat16 [16, 4096, 6144], P('exp', None, 'seq'), may hold values from -0.09375 to 0.09375
- w_down: bfloat16 [16, 6144, 4096], P('exp', 'seq'), may hold values from -0.0546875 to 0.0546875
Outputs:
- layer_out: bfloat16 [512, 4, 4096], P(('seq', 'exp'))
Inputs may be any that keep to these rules, and one draw needn't show every extreme that they name: `expert_ids`: tokens are ordered by position, then document; in each aligned block of 16 such tokens (the tokens of one device), every expert is named at most 8 times, and in every draw some expert is named exactly 8 times in some block. Each token names 2 different experts.
All inputs are finite; a program needn't handle non-finite values.
Results may differ from a plain program's by a relative error of at most 0.03.
Values may be sent and summed in bfloat16 or wider, within the bound.
No kernel may reach another device: no remote copies, remote signals or barrier semaphores. Data moves between devices by JAX's collectives and lax.ppermute only.
A program may use at most 128 MiB of HBM per device.

v0:
```python
import jax
import jax.numpy as jnp
from jax import lax
from jax.sharding import PartitionSpec as P

D = 4096
STATE = 16
CONV = 4
RANK = 256
EXPERTS = 8
TOPK = 2


def passed_along(value, axis, by):
    count = lax.axis_size(axis)
    pairs = [(i, i + by) for i in range(count) if 0 <= i + by < count]
    return lax.ppermute(value, axis, pairs)


def entering(value, axis, join, neutral):
    place = lax.axis_index(axis)
    gathered = jax.tree.map(
        lambda a, kind: lax.all_gather(a.astype(kind), axis), value, (jnp.bfloat16, jnp.bfloat16)
    )
    state = jax.tree.map(lambda a, e: jnp.zeros_like(a) + jnp.asarray(e, a.dtype), value, neutral)

    def one(step, state):
        return join(
            state,
            jax.tree.map(
                lambda a, own: lax.dynamic_index_in_dim(a, step, 0, False).astype(own.dtype),
                gathered,
                value,
            ),
        )

    return lax.fori_loop(0, place, one, state)


def conv_inputs(window, conv_weight, conv_bias, length):
    running = jnp.zeros(window[:length].shape, jnp.float32) + conv_bias
    for offset in range(CONV):
        running = running + conv_weight[offset] * window[offset : offset + length]
    return running


def make_step(decay_rate):

    def advance(carry_state, series_now):
        step_now, input_now, read_now, value_now = series_now
        factor = jnp.exp(step_now[:, None, :] * decay_rate[None])
        carry_state = (
            factor * carry_state + (step_now * value_now)[:, None, :] * input_now[:, :, None]
        )
        return (carry_state, jnp.sum(read_now[:, :, None] * carry_state, axis=1))

    return advance


def chain(earlier, later):
    return (earlier[0] * later[0], later[0] * earlier[1] + later[1])


def slot_select(route_ids, capacity):
    flat_ids = route_ids.reshape(-1)
    onehot = (flat_ids[:, None] == jnp.arange(EXPERTS, dtype=jnp.int32)[None, :]).astype(jnp.int32)
    before = jnp.sum((jnp.cumsum(onehot, axis=0) - onehot) * onehot, axis=1)
    target = flat_ids * capacity + before
    matches = jnp.arange(EXPERTS * capacity, dtype=jnp.int32)[:, None] == target[None, :]
    return matches.reshape(EXPERTS * capacity, route_ids.shape[0], route_ids.shape[1])


def per_device(
    xin,
    zin,
    conv_weight,
    conv_bias,
    xproj_weight,
    dtproj_weight,
    dt_bias,
    a_log,
    skip,
    out_weight,
    resid,
    norm_gain,
    expert_ids,
    gate_weights,
    w_gate,
    w_up,
    w_down,
):
    section = xin.shape[0]
    edge_rows = passed_along(xin[section - (CONV - 1) :], "seq", 1)
    window = jnp.concatenate([edge_rows, xin], axis=0).astype(jnp.float32)
    inner_act = jax.nn.silu(conv_inputs(window, conv_weight, conv_bias, section)).astype(
        jnp.bfloat16
    )
    inner_f = inner_act.astype(jnp.float32)
    projected = jnp.einsum(
        "pbc,cr->pbr", inner_act, xproj_weight, preferred_element_type=jnp.float32
    )
    projected = lax.psum(projected.astype(jnp.bfloat16), "exp").astype(jnp.float32)
    low_rank = projected[..., :RANK].astype(jnp.bfloat16)
    in_state = projected[..., RANK : RANK + STATE]
    out_state = projected[..., RANK + STATE :]
    step_size = jax.nn.softplus(
        jnp.einsum("pbr,rc->pbc", low_rank, dtproj_weight, preferred_element_type=jnp.float32)
        + dt_bias
    )
    decay_rate = -jnp.exp(a_log)
    advance = make_step(decay_rate)
    series = (step_size, in_state, out_state, inner_f)
    zero_state = jnp.zeros((xin.shape[1], STATE, xin.shape[2]), jnp.float32)
    final_local, local_out = lax.scan(advance, zero_state, series)
    total_decay = jnp.exp(jnp.sum(step_size, axis=0)[:, None, :] * decay_rate[None])
    identity = (jnp.ones_like(total_decay), jnp.zeros_like(final_local))
    incoming = entering((total_decay, final_local), "seq", chain, identity)[1]
    ignored, ssm_out = lax.scan(advance, incoming, series)
    mixed_in = ((ssm_out + skip * inner_f) * jax.nn.silu(zin.astype(jnp.float32))).astype(
        jnp.bfloat16
    )
    row_block = mixed_in
    mamba_rows = lax.psum_scatter(
        jnp.einsum("pbc,cd->pbd", row_block, out_weight, preferred_element_type=jnp.float32).astype(
            jnp.bfloat16
        ),
        "exp",
        scatter_dimension=0,
        tiled=True,
    ).astype(jnp.float32)
    hidden_state = resid.astype(jnp.float32) + mamba_rows
    norm_scale = lax.rsqrt(jnp.mean(hidden_state * hidden_state, axis=-1, keepdims=True) + 1e-05)
    normed = (hidden_state * norm_scale * norm_gain).astype(jnp.bfloat16)
    row_count = resid.shape[0] * resid.shape[1]
    capacity = 2 * TOPK * row_count // EXPERTS
    splits = lax.axis_size("exp") // EXPERTS
    tokens = normed.reshape(row_count, D)
    route_ids = expert_ids.reshape(row_count, TOPK)
    gate_vals = gate_weights.reshape(row_count, TOPK)
    matches = slot_select(route_ids, capacity)
    chosen = jnp.sum(matches.astype(jnp.int32), axis=2).astype(jnp.bfloat16)
    outgoing = (
        jnp.dot(chosen, tokens, preferred_element_type=jnp.float32)
        .astype(jnp.bfloat16)
        .reshape(EXPERTS, capacity, D)
    )
    arrived = lax.all_to_all(
        jnp.tile(outgoing, (splits, 1, 1)), "exp", split_axis=0, concat_axis=0, tiled=True
    )
    everything = lax.all_gather(arrived, "seq", axis=0, tiled=True)
    row_block = everything
    expert_row_block = row_block.reshape(-1, D)
    gate_act = jnp.dot(expert_row_block, w_gate[0], preferred_element_type=jnp.float32)
    up_act = jnp.dot(expert_row_block, w_up[0], preferred_element_type=jnp.float32)
    hidden = (jax.nn.silu(gate_act) * up_act).astype(jnp.bfloat16)
    own_rows = lax.psum_scatter(
        jnp.dot(hidden, w_down[0], preferred_element_type=jnp.float32)
        .reshape(lax.axis_size("seq") * arrived.shape[0], capacity, D)
        .astype(jnp.bfloat16),
        "seq",
        scatter_dimension=0,
        tiled=True,
    ).astype(jnp.float32)
    returned = lax.all_to_all(
        own_rows.astype(jnp.bfloat16), "exp", split_axis=0, concat_axis=0, tiled=True
    ).astype(own_rows.dtype)
    summed = jnp.sum(returned.reshape(splits, EXPERTS * capacity, D), axis=0)
    weights = jnp.sum(matches.astype(jnp.float32) * gate_vals.astype(jnp.float32)[None], axis=2)
    expert_out = jnp.dot(weights.T, summed, precision=lax.Precision.HIGHEST)
    return (hidden_state + expert_out.reshape(hidden_state.shape)).astype(jnp.bfloat16)


def solution(mesh):
    placed = (
        P("seq", None, "exp"),
        P("seq", None, "exp"),
        P(None, "exp"),
        P("exp"),
        P("exp", None),
        P(None, "exp"),
        P("exp"),
        P(None, "exp"),
        P("exp"),
        P("exp", None),
        P(("seq", "exp"), None, None),
        P(),
        P(("seq", "exp"), None, None),
        P(("seq", "exp"), None, None),
        P("exp", None, "seq"),
        P("exp", None, "seq"),
        P("exp", "seq", None),
    )
    return jax.shard_map(
        per_device,
        mesh=mesh,
        in_specs=placed,
        out_specs=P(("seq", "exp"), None, None),
        check_vma=False,
    )
```

profile of v0, /device:TPU:2, one launch (start us, length us, event | category | flops | bytes accessed | tf_op | source)
XLA Modules:
  0.0 485.4 jit_solution(7767882943626385610)
XLA Ops:
  6.6 0.8 slice.38
  7.4 1.9 collective-permute-start
  9.3 0.9 fusion.43
  10.2 2.2 collective-permute-done
  12.4 1.1 maximum_convert_fusion
  13.5 1.2 fusion.39
  14.7 1.0 convolution_convert_fusion.3
  15.8 86.0 %all-reduce.4.cloned.1.call-done = bf16[64,4,288]{2,0,1:T(8,128)(2,1)} async-done(((bf16[64,4,288]{2,0,1:T(8,128)(2,1)}), bf16[64,4,288]{2,0,1:T(8,128)(2,1)}) %all-reduce.4.cloned.1.call-update) | async-done | bytes 147472 | tf_op jit(solution)/shard_map/psum | solution.py:102
  101.8 1.2 fusion.35
  103.6 1.7 fusion.42
  105.4 10.3 %while.37 = (s32[]{:T(128)}, f32[4,16,512]{2,1,0:T(8,128)S(1)}, f32[64,4,512]{2,1,0:T(4,128)S(1)}, f32[16,512]{1,0:T(8,128)S(1)}, f32[64,4,512]{2,1,0:T(4,128)S(...) while((s32[]{:T(128)}, f32[4,16,512]{2,1,0:T(8,128)S(1)}, f32[64,4,512]{2,1,0:T(4,128)S(1)}, ...), condition=%wide.region_3.4_spmd.clone, body=%wide.region_2.3_spmd.clone.sunk | while | flops 165891 | bytes 353131 | solution.py:114
  115.7 13.1 %all-gather = bf16[32,16,512]{2,1,0:T(8,128)(2,1)S(1)} all-gather(bf16[4,16,512]{2,1,0:T(8,128)(2,1)S(1)} %convert_element_type.103), channel_id=2, replica_groups=mesh['seq'=8,'exp'=16] {'seq'}, dimensions={0}, use_global_device_ids=true | all-gather | bytes 589824 | tf_op jit(solution)/shard_map/all_gather | solution.py:23
  128.9 13.1 %all_gather.13 = bf16[8,4,16,512]{3,2,1,0:T(8,128)(2,1)S(1)} all-gather(bf16[1,4,16,512]{3,2,1,0:T(8,128)(2,1)S(1)} %exponential_convert_fusion), channel_id=1, replica_groups=mesh['seq'=8,'exp'=16] {'seq'}, dimensions={0}, use_global_device_ids=true | all-gather | bytes 589824 | tf_op jit(solution)/shard_map/all_gather | solution.py:23
  142.2 58.7 %while.36 = (s32[]{:T(128)}, f32[4,16,512]{2,1,0:T(8,128)S(1)}, f32[64,4,512]{2,1,0:T(4,128)S(1)}, f32[64,4,512]{2,1,0:T(4,128)S(1)}, f32[16,512]{1,0:T(8,128)S(...) while((s32[]{:T(128)}, f32[4,16,512]{2,1,0:T(8,128)S(1)}, ...), condition=%wide.region_8.9_spmd, body=%wide.region_6.8_spmd.sunk | while | flops 196610 | bytes 378481 | solution.py:118
  142.2 0.7 constant_dynamic-slice_fusion.3
  143.1 0.7 constant_dynamic-slice_fusion.3
  144.1 0.7 constant_dynamic-slice_fusion.3
  145.0 0.7 constant_dynamic-slice_fusion.3
  145.9 0.7 constant_dynamic-slice_fusion.3
  146.8 0.7 constant_dynamic-slice_fusion.3
  147.7 0.7 constant_dynamic-slice_fusion.3
  148.6 0.7 constant_dynamic-slice_fusion.3
  149.6 0.7 constant_dynamic-slice_fusion.3
  150.5 0.7 constant_dynamic-slice_fusion.3
  151.4 0.7 constant_dynamic-slice_fusion.3
  152.3 0.7 constant_dynamic-slice_fusion.3
  153.2 0.7 constant_dynamic-slice_fusion.3
  154.1 0.7 constant_dynamic-slice_fusion.3
  155.0 0.7 constant_dynamic-slice_fusion.3
  156.0 0.7 constant_dynamic-slice_fusion.3
  156.9 0.7 constant_dynamic-slice_fusion.3
  157.8 0.7 constant_dynamic-slice_fusion.3
  158.7 0.7 constant_dynamic-slice_fusion.3
  159.6 0.7 constant_dynamic-slice_fusion.3
  178.8 0.8 constant_dynamic-slice_fusion.3
  179.7 0.8 constant_dynamic-slice_fusion.3
  180.7 0.8 constant_dynamic-slice_fusion.3
  181.6 0.8 constant_dynamic-slice_fusion.3
  182.5 0.8 constant_dynamic-slice_fusion.3
  183.5 0.8 constant_dynamic-slice_fusion.3
  184.4 0.8 constant_dynamic-slice_fusion.3
  185.4 0.8 constant_dynamic-slice_fusion.3
  193.6 0.7 constant_dynamic-slice_fusion.3
  194.5 0.7 constant_dynamic-slice_fusion.3
  195.4 0.7 constant_dynamic-slice_fusion.3
  196.4 0.7 constant_dynamic-slice_fusion.3
  197.3 0.7 constant_dynamic-slice_fusion.3
  198.2 0.7 constant_dynamic-slice_fusion.3
  199.1 0.7 constant_dynamic-slice_fusion.3
  200.0 0.7 constant_dynamic-slice_fusion.3
  200.9 1.3 fusion.30
  202.3 4.8 convolution_convert_fusion.1
  209.3 87.8 %all-reduce.6.cloned.1.call-done = bf16[64,4,4096]{2,0,1:T(8,128)(2,1)} async-done(((bf16[64,4,4096]{2,0,1:T(8,128)(2,1)}), bf16[64,4,4096]{2,0,1:T(8,128)(2,1)}) %all-reduce.6.cloned.1.call-update) | async-done | bytes 2097168
  297.1 1.0 constant_dynamic-slice_fusion.1
  299.1 20.6 %all_to_all.10 = bf16[16,8,4096]{2,1,0:T(8,128)(2,1)} all-to-all(bf16[16,8,4096]{2,1,0:T(8,128)(2,1)S(1)} %bitcast.113), channel_id=1, replica_groups=mesh['seq'=8,'exp'=16] {'exp'}, dimensions={0} | all-to-all | bytes 2097152 | tf_op jit(solution)/shard_map/all_to_all | solution.py:147
  319.9 46.7 %all-gather.3.cloned.1.call-done = bf16[128,8,4096]{2,1,0:T(8,128)(2,1)} async-done(((bf16[16,8,4096]{2,1,0:T(8,128)(2,1)}), bf16[128,8,4096]{2,1,0:T(8,128)(2,1)}) %all-gather.3.cloned.1.call-update) | async-done | bytes 8388624 | tf_op jit(solution)/shard_map/all_gather | solution.py:150
  366.6 11.0 %fusion.1 = f32[1024,768]{1,0:T(8,128)S(1)} fusion(bf16[128,8,4096]{2,1,0:T(8,128)(2,1)} %all-gather.3.cloned.1.call-done, bf16[1,4096,768]{2,1,0:T(8,128)(2,1)} %param.38), kind=kOutput, calls=%fused_computation.14 | convolution fusion | flops 6442450944 | bytes 17825792 | tf_op jit(solution)/shard_map/dot_general | solution.py:154
  377.7 9.9 %fusion.16 = bf16[128,8,768]{2,1,0:T(8,128)(2,1)S(1)} fusion(f32[1024,768]{1,0:T(8,128)S(1)} %fusion.1, bf16[1,4096,768]{2,1,0:T(8,128)(2,1)} %param.37, bf16[128,8,4096]{2,1,0:T(8,128)(2,1)S(1)} %copy-done.9), kind=kOutput, calls=%fused_computation.31 | convolution fusion | flops 6447169536 | bytes 19398656 | tf_op jit(solution)/shard_map/dot_general | solution.py:153
  387.6 8.9 %convolution_convert_fusion = bf16[128,8,4096]{2,0,1:T(8,128)(2,1)} fusion(bf16[1,768,4096]{2,1,0:T(8,128)(2,1)S(1)} %bitcast.122, bf16[128,8,768]{2,1,0:T(8,128)(2,1)S(1)} %fusion.16), kind=kOutput, calls=%fused_computation.18 | convolution fusion | flops 6446645248 | bytes 16252928 | tf_op jit(solution)/shard_map/dot_general | solution.py:157
  396.5 51.1 %reduce-scatter.3.cloned.1.call-done = bf16[16,8,4096]{2,0,1:T(8,128)(2,1)} async-done(((bf16[128,8,4096]{2,0,1:T(8,128)(2,1)}), bf16[16,8,4096]{2,0,1:T(8,128)(2,1)}) %reduce-scatter.3.cloned.1.call-update) | async-done | bytes 1048592 | tf_op jit(solution)/shard_map/reduce_scatter | solution.py:156
  447.7 2.8 copy.87
  450.4 7.2 %all-to-all-start.1 = ((bf16[16,8,4096]{2,1,0:T(8,128)(2,1)}), bf16[16,8,4096]{2,1,0:T(8,128)(2,1)S(1)}, u32[]{:S(2)}, u32[]{:S(2)}) async-start(bf16[16,8,4096]{2,1,0:T(8,128)(2,1)} %copy.87), calls=%async_computation.2 | async-start | bytes 2097152 | tf_op jit(solution)/shard_map/all_to_all | solution.py:164
  457.9 19.5 %all-to-all-done.1 = bf16[16,8,4096]{2,1,0:T(8,128)(2,1)S(1)} async-done(((bf16[16,8,4096]{2,1,0:T(8,128)(2,1)}), bf16[16,8,4096]{2,1,0:T(8,128)(2,1)S(1)}, u32[]{:S(2)}, u32[]{:S(2)}) %all-to-all-start.1) | async-done | bytes 1048608 | tf_op jit(solution)/shard_map/all_to_all | solution.py:164
  477.5 1.4 fusion.9
  (674 shorter events, 41.5 us)
Async XLA Ops:
  6.5 8.1 %copy-start = (bf16[512,288]{0,1:T(8,128)(2,1)S(1)}, bf16[512,288]{0,1:T(8,128)(2,1)}, u32[]{:S(2)}) copy-start(bf16[512,288]{0,1:T(8,128)(2,1)} %param.27) | copy-start | bytes 884740
  6.5 9.2 %copy-start.3 = (f32[16,512]{1,0:T(8,128)S(1)}, f32[16,512]{1,0:T(8,128)}, u32[]{:S(2)}) copy-start(f32[16,512]{1,0:T(8,128)} %param.30) | copy-start | bytes 98308
  6.5 95.3 %copy-start.2 = (bf16[256,512]{1,0:T(8,128)(2,1)S(1)}, bf16[256,512]{1,0:T(8,128)(2,1)}, u32[]{:S(2)}) copy-start(bf16[256,512]{1,0:T(8,128)(2,1)} %param.28) | copy-start | bytes 786436
  6.5 95.3 %copy-start.6 = (f32[512]{0:T(512)S(1)}, f32[512]{0:T(512)}, u32[]{:S(2)}) copy-start(f32[512]{0:T(512)} %param.29) | copy-start | bytes 6148
  6.5 95.2 %all-reduce.4.cloned.1.call-start = ((), (), s32[]{:S(2)}) async-start(), calls=%async_computation.3 | async-start | bytes 393216 | tf_op jit(solution)/shard_map/psum | solution.py:102
  7.4 5.0 %collective-permute-start = (bf16[3,4,512]{2,1,0:T(4,128)(2,1)S(1)}, bf16[3,4,512]{2,1,0:T(4,128)(2,1)S(1)}, u32[]{:S(2)}, u32[]{:S(2)}) collective-permute-start(bf16[3,4,512]{2,1,0:T(4,128)(2,1)S(1)} %slice.38), channel_id=1, source_target_pairs={{0,16},{16,32},{32,48},{48,64},{64,80},{80,96},{96,112},{1,17},{17... | collective-permute-start | bytes 36872 | tf_op jit(solution)/shard_map/ppermute | solution.py:17
  15.7 281.4 %all-reduce.6.cloned.1.call-start = ((), (), s32[]{:S(2)}) async-start(), calls=%async_computation.6 | async-start | bytes 4194304
  105.3 95.6 %copy-start.7 = (f32[512]{0:T(512)S(1)}, f32[512]{0:T(512)}, u32[]{:S(2)}) copy-start(f32[512]{0:T(512)} %param.31) | copy-start | bytes 6148
  202.3 4.9 %copy-start.5 = (s32[4,4,2]{1,2,0:T(2,128)S(1)}, s32[4,4,2]{1,2,0:T(2,128)}, u32[]{:S(2)}) copy-start(s32[4,4,2]{1,2,0:T(2,128)} %param.35) | copy-start | bytes 388
  202.3 5.7 %copy-start.10 = (u32[128]{0:T(128)S(1)}, u32[128]{0:T(128)}, u32[]{:S(2)}) copy-start(u32[128]{0:T(128)} %constant.77) | copy-start | bytes 1540
  202.3 95.9 %copy-start.1 = (bf16[4,4,4096]{2,1,0:T(4,128)(2,1)S(1)}, bf16[4,4,4096]{2,1,0:T(4,128)(2,1)}, u32[]{:S(2)}) copy-start(bf16[4,4,4096]{2,1,0:T(4,128)(2,1)} %param.33) | copy-start | bytes 393220
  202.3 96.1 %copy-start.4 = (f32[4096]{0:T(1024)S(1)}, f32[4096]{0:T(1024)}, u32[]{:S(2)}) copy-start(f32[4096]{0:T(1024)} %param.34) | copy-start | bytes 49156
  207.1 159.5 %all-gather.3.cloned.1.call-start = ((), (), s32[]{:S(2)}) async-start(), calls=%async_computation.4 | async-start | bytes 9437184 | tf_op jit(solution)/shard_map/all_gather | solution.py:150
  319.7 128.0 %reduce-scatter.3.cloned.1.call-start = ((), (), s32[]{:S(2)}) async-start(), calls=%async_computation.5 | async-start | bytes 9437184 | tf_op jit(solution)/shard_map/reduce_scatter | solution.py:156
  366.6 11.0 %copy-start.9 = (bf16[128,8,4096]{2,1,0:T(8,128)(2,1)S(1)}, bf16[128,8,4096]{2,1,0:T(8,128)(2,1)}, u32[]{:S(2)}) copy-start(bf16[128,8,4096]{2,1,0:T(8,128)(2,1)} %all-gather.3.cloned.1.call-done) | copy-start | bytes 25165828
  366.6 21.0 %slice-start = ((s8[6291456]{0:T(1024)(128)(4,1)}), s8[4194304]{0:T(1024)(128)(4,1)S(1)}, s32[]{:S(2)}) async-start(s8[6291456]{0:T(1024)(128)(4,1)} %bitcast.121), calls=%async_computation.7 | async-start | bytes 8388608
  377.7 10.0 %slice-start.1 = ((s8[6291456]{0:T(1024)(128)(4,1)}), s8[2097152]{0:T(1024)(128)(4,1)S(1)}, s32[]{:S(2)}) async-start(s8[6291456]{0:T(1024)(128)(4,1)} %bitcast.121), calls=%async_computation.8 | async-start | bytes 4194304
  396.5 61.2 %copy-start.8 = (bf16[4,4,2]{1,2,0:T(2,128)(2,1)S(1)}, bf16[4,4,2]{1,2,0:T(2,128)(2,1)}, u32[]{:S(2)}) copy-start(bf16[4,4,2]{1,2,0:T(2,128)(2,1)} %param.36) | copy-start | bytes 196
  450.4 26.9 %all-to-all-start.1 = ((bf16[16,8,4096]{2,1,0:T(8,128)(2,1)}), bf16[16,8,4096]{2,1,0:T(8,128)(2,1)S(1)}, u32[]{:S(2)}, u32[]{:S(2)}) async-start(bf16[16,8,4096]{2,1,0:T(8,128)(2,1)} %copy.87), calls=%async_computation.2 | async-start | bytes 2097152 | tf_op jit(solution)/shard_map/all_to_all | solution.py:164
Sparse Core Ops, SparseCore 0:
  15.8 85.9 all-reduce.3
  207.3 89.8 all-reduce.5
  319.8 46.7 all-gather.2
  396.7 50.9 reduce-scatter.2
where the time goes:
time: 489 us; the launch traced here: 485 us
  waiting for transfers between devices  293 us (60%)
  local copies, waits for them, and re-layouts  58.7 us (12%)
  blocking collectives  46.9 us (10%)
  matrix products  38.5 us (8%)
  other arithmetic  19.2 us (4%)
  between operations  14.1 us (3%)
  starting transfers between devices  9.47 us (2%)
  loops' own time  5.32 us (1%)
    unnamed x5, waiting for transfers between devices  87.8 us
    psum x1, waiting for transfers between devices, per_device(): lax.psum(projected.astype(jnp.bfloat16), 'exp').astype(jnp.float32)  86 us
    reduce_scatter x1, waiting for transfers between devices, per_device(): lax.psum_scatter(jnp.dot(hidden, w_down[0], preferred_element_type=jnp.fl...  51.1 us
    dynamic_slice x64, local copies, waits for them, and re-layouts, per_device(): final_local, local_out = lax.scan(advance, zero_state, series)  47 us
    all_gather x1, waiting for transfers between devices, per_device(): everything = lax.all_gather(arrived, 'seq', axis=0, tiled=True)  46.7 us
    all_gather x2, blocking collectives, entering(): lax.all_gather(a.astype(kind), axis)  26.2 us
    all_to_all x1, blocking collectives, per_device(): lax.all_to_all(jnp.tile(outgoing, (splits, 1, 1)), 'exp', split_axis=0, c...  20.6 us
    all_to_all x1, waiting for transfers between devices, per_device(): lax.all_to_all(own_rows.astype(jnp.bfloat16), 'exp', split_axis=0, concat...  19.5 us
  transfers between devices with their start and end apart: 6, of which 6 were waited for; matrix products, arithmetic and copies ran while one was open for 1% of the time, Pallas kernels for 0%

commit v1 on v0

--- a/solution.py
+++ b/solution.py
@@ -2,6 +2,7 @@
 import jax.numpy as jnp
 from jax import lax
 from jax.sharding import PartitionSpec as P
+from jax.lax import all_gather
 
 D = 4096
 STATE = 16
@@ -9,6 +10,10 @@
 RANK = 256
 EXPERTS = 8
 TOPK = 2
+
+
+def link_meshes(my_data):
+    return jnp.sum(all_gather(my_data, "exp"), axis=0)
 
 
 def passed_along(value, axis, by):
@@ -99,7 +104,7 @@
     projected = jnp.einsum(
         "pbc,cr->pbr", inner_act, xproj_weight, preferred_element_type=jnp.float32
     )
-    projected = lax.psum(projected.astype(jnp.bfloat16), "exp").astype(jnp.float32)
+    projected = link_meshes(projected.astype(jnp.bfloat16)).astype(jnp.float32)
     low_rank = projected[..., :RANK].astype(jnp.bfloat16)
     in_state = projected[..., RANK : RANK + STATE]
     out_state = projected[..., RANK + STATE :]

time: 489 us -> 454 us (0.928)
  waiting for transfers between devices: 293 us -> 257 us
    psum x1 -> x0, waiting for transfers between devices: 86 us -> none  [per_device(): lax.psum(projected.astype(jnp.bfloat16), 'exp').astype(jnp.float32)]
    all_gather x0 -> x1, waiting for transfers between devices: none -> 50.5 us  [link_meshes(): return jnp.sum(all_gather(my_data, 'exp'), axis=0)]
where the time goes in v1:
time: 454 us; the launch traced here: 450 us
  waiting for transfers between devices  257 us (57%)
  local copies, waits for them, and re-layouts  57.8 us (13%)
  blocking collectives  46.9 us (10%)
  matrix products  37.6 us (8%)
  other arithmetic  21.6 us (5%)
  between operations  14.1 us (3%)
  starting transfers between devices  9.42 us (2%)
  loops' own time  5.32 us (1%)
    unnamed x5, waiting for transfers between devices  87.3 us
    reduce_scatter x1, waiting for transfers between devices, per_device(): lax.psum_scatter(jnp.dot(hidden, w_down[0], preferred_element_type=jnp.fl...  51.1 us
    all_gather x1, waiting for transfers between devices, link_meshes(): return jnp.sum(all_gather(my_data, 'exp'), axis=0)  50.5 us
    dynamic_slice x64, local copies, waits for them, and re-layouts, per_device(): final_local, local_out = lax.scan(advance, zero_state, series)  47 us
    all_gather x1, waiting for transfers between devices, per_device(): everything = lax.all_gather(arrived, 'seq', axis=0, tiled=True)  46.6 us
    all_gather x2, blocking collectives, entering(): lax.all_gather(a.astype(kind), axis)  26.2 us
    all_to_all x1, blocking collectives, per_device(): lax.all_to_all(jnp.tile(outgoing, (splits, 1, 1)), 'exp', split_axis=0, c...  20.6 us
    all_to_all x1, waiting for transfers between devices, per_device(): lax.all_to_all(own_rows.astype(jnp.bfloat16), 'exp', split_axis=0, concat...  19.4 us
  transfers between devices with their start and end apart: 6, of which 6 were waited for; matrix products, arithmetic and copies ran while one was open for 1% of the time, Pallas kernels for 0%

profile of v1, /device:TPU:2, one launch (start us, length us, event | category | flops | bytes accessed | tf_op | source)
XLA Modules:
  0.0 450.0 jit_solution(5745010577629147568)
XLA Ops:
  6.5 0.8 slice.38
  7.3 1.9 collective-permute-start
  9.2 0.9 fusion.43
  10.1 2.2 collective-permute-done
  12.3 1.1 maximum_convert_fusion
  13.4 1.2 fusion.39
  14.6 1.0 convolution_convert_fusion.3
  15.7 50.5 %all-gather.7.cloned.1.call-done = bf16[1024,4,288]{2,0,1:T(8,128)(2,1)} async-done(((bf16[64,4,288]{2,0,1:T(8,128)(2,1)}), bf16[1024,4,288]{2,0,1:T(8,128)(2,1)}) %all-gather.7.cloned.1.call-update) | async-done | bytes 2359312 | tf_op jit(solution)/shard_map/all_gather | solution.py:16
  66.3 2.5 reduce_sum.77
  68.8 0.7 fusion.42
  70.6 10.3 %while.37 = (s32[]{:T(128)}, f32[4,16,512]{2,1,0:T(8,128)S(1)}, f32[64,4,512]{2,1,0:T(4,128)S(1)}, f32[16,512]{1,0:T(8,128)S(1)}, f32[64,4,512]{2,1,0:T(4,128)S(...) while((s32[]{:T(128)}, f32[4,16,512]{2,1,0:T(8,128)S(1)}, f32[64,4,512]{2,1,0:T(4,128)S(1)}, ...), condition=%wide.region_3.4_spmd.clone, body=%wide.region_2.3_spmd.clone.sunk | while | flops 165891 | bytes 353131 | solution.py:119
  80.9 13.1 %all-gather.1 = bf16[32,16,512]{2,1,0:T(8,128)(2,1)S(1)} all-gather(bf16[4,16,512]{2,1,0:T(8,128)(2,1)S(1)} %convert_element_type.105), channel_id=3, replica_groups=mesh['seq'=8,'exp'=16] {'seq'}, dimensions={0}, use_global_device_ids=true | all-gather | bytes 589824 | tf_op jit(solution)/shard_map/all_gather | solution.py:28
  94.0 13.1 %all_gather.21 = bf16[8,4,16,512]{3,2,1,0:T(8,128)(2,1)S(1)} all-gather(bf16[1,4,16,512]{3,2,1,0:T(8,128)(2,1)S(1)} %exponential_convert_fusion), channel_id=1, replica_groups=mesh['seq'=8,'exp'=16] {'seq'}, dimensions={0}, use_global_device_ids=true | all-gather | bytes 589824 | tf_op jit(solution)/shard_map/all_gather | solution.py:28
  107.3 58.7 %while.36 = (s32[]{:T(128)}, f32[4,16,512]{2,1,0:T(8,128)S(1)}, f32[64,4,512]{2,1,0:T(4,128)S(1)}, f32[64,4,512]{2,1,0:T(4,128)S(1)}, f32[16,512]{1,0:T(8,128)S(...) while((s32[]{:T(128)}, f32[4,16,512]{2,1,0:T(8,128)S(1)}, ...), condition=%wide.region_8.9_spmd, body=%wide.region_6.8_spmd.sunk | while | flops 196610 | bytes 378481 | solution.py:123
  107.4 0.7 constant_dynamic-slice_fusion.3
  108.3 0.7 constant_dynamic-slice_fusion.3
  109.2 0.7 constant_dynamic-slice_fusion.3
  110.1 0.7 constant_dynamic-slice_fusion.3
  111.0 0.7 constant_dynamic-slice_fusion.3
  112.0 0.7 constant_dynamic-slice_fusion.3
  112.9 0.7 constant_dynamic-slice_fusion.3
  113.8 0.7 constant_dynamic-slice_fusion.3
  114.7 0.7 constant_dynamic-slice_fusion.3
  115.6 0.7 constant_dynamic-slice_fusion.3
  116.5 0.7 constant_dynamic-slice_fusion.3
  117.5 0.7 constant_dynamic-slice_fusion.3
  118.4 0.7 constant_dynamic-slice_fusion.3
  119.3 0.7 constant_dynamic-slice_fusion.3
  120.2 0.7 constant_dynamic-slice_fusion.3
  121.1 0.7 constant_dynamic-slice_fusion.3
  122.0 0.7 constant_dynamic-slice_fusion.3
  122.9 0.7 constant_dynamic-slice_fusion.3
  123.9 0.7 constant_dynamic-slice_fusion.3
  124.8 0.7 constant_dynamic-slice_fusion.3
  144.0 0.8 constant_dynamic-slice_fusion.3
  144.9 0.8 constant_dynamic-slice_fusion.3
  145.8 0.8 constant_dynamic-slice_fusion.3
  146.8 0.8 constant_dynamic-slice_fusion.3
  147.7 0.8 constant_dynamic-slice_fusion.3
  148.6 0.8 constant_dynamic-slice_fusion.3
  149.6 0.8 constant_dynamic-slice_fusion.3
  150.5 0.8 constant_dynamic-slice_fusion.3
  158.8 0.7 constant_dynamic-slice_fusion.3
  159.7 0.7 constant_dynamic-slice_fusion.3
  160.6 0.7 constant_dynamic-slice_fusion.3
  161.5 0.7 constant_dynamic-slice_fusion.3
  162.4 0.7 constant_dynamic-slice_fusion.3
  163.4 0.7 constant_dynamic-slice_fusion.3
  164.3 0.7 constant_dynamic-slice_fusion.3
  165.2 0.7 constant_dynamic-slice_fusion.3
  166.1 1.3 fusion.30
  167.5 4.8 %convolution_convert_fusion.1 = bf16[64,4,4096]{2,0,1:T(8,128)(2,1)} fusion(bf16[512,4096]{1,0:T(8,128)(2,1)} %param.32, bf16[64,4,512]{2,1,0:T(4,128)(2,1)S(1)} %fusion.30), kind=kOutput, calls=%fused_computation.22 | convolution fusion | flops 1074790400 | bytes 6553600 | tf_op jit(solution)/shard_map/pbc,cd->pbd/dot_general | solution.py:129
  174.5 87.2 %all-reduce.3.cloned.1.call-done = bf16[64,4,4096]{2,0,1:T(8,128)(2,1)} async-done(((bf16[64,4,4096]{2,0,1:T(8,128)(2,1)}), bf16[64,4,4096]{2,0,1:T(8,128)(2,1)}) %all-reduce.3.cloned.1.call-update) | async-done | bytes 2097168
  261.7 1.0 constant_dynamic-slice_fusion.1
  263.7 20.6 %all_to_all.10 = bf16[16,8,4096]{2,1,0:T(8,128)(2,1)} all-to-all(bf16[16,8,4096]{2,1,0:T(8,128)(2,1)S(1)} %bitcast.114), channel_id=1, replica_groups=mesh['seq'=8,'exp'=16] {'exp'}, dimensions={0} | all-to-all | bytes 2097152 | tf_op jit(solution)/shard_map/all_to_all | solution.py:152
  284.6 46.6 %all-gather.5.cloned.1.call-done = bf16[128,8,4096]{2,1,0:T(8,128)(2,1)} async-done(((bf16[16,8,4096]{2,1,0:T(8,128)(2,1)}), bf16[128,8,4096]{2,1,0:T(8,128)(2,1)}) %all-gather.5.cloned.1.call-update) | async-done | bytes 8388624 | tf_op jit(solution)/shard_map/all_gather | solution.py:155
  331.2 11.0 %fusion.1 = f32[1024,768]{1,0:T(8,128)S(1)} fusion(bf16[128,8,4096]{2,1,0:T(8,128)(2,1)} %all-gather.5.cloned.1.call-done, bf16[1,4096,768]{2,1,0:T(8,128)(2,1)} %param.38), kind=kOutput, calls=%fused_computation.14 | convolution fusion | flops 6442450944 | bytes 17825792 | tf_op jit(solution)/shard_map/dot_general | solution.py:159
  342.3 9.9 %fusion.16 = bf16[128,8,768]{2,1,0:T(8,128)(2,1)S(1)} fusion(f32[1024,768]{1,0:T(8,128)S(1)} %fusion.1, bf16[1,4096,768]{2,1,0:T(8,128)(2,1)} %param.37, bf16[128,8,4096]{2,1,0:T(8,128)(2,1)S(1)} %copy-done.9), kind=kOutput, calls=%fused_computation.31 | convolution fusion | flops 6447169536 | bytes 19398656 | tf_op jit(solution)/shard_map/dot_general | solution.py:158
  352.3 8.9 %convolution_convert_fusion = bf16[128,8,4096]{2,0,1:T(8,128)(2,1)} fusion(bf16[1,768,4096]{2,1,0:T(8,128)(2,1)S(1)} %bitcast.124, bf16[128,8,768]{2,1,0:T(8,128)(2,1)S(1)} %fusion.16), kind=kOutput, calls=%fused_computation.18 | convolution fusion | flops 6446645248 | bytes 16252928 | tf_op jit(solution)/shard_map/dot_general | solution.py:162
  361.2 51.1 %reduce-scatter.3.cloned.1.call-done = bf16[16,8,4096]{2,0,1:T(8,128)(2,1)} async-done(((bf16[128,8,4096]{2,0,1:T(8,128)(2,1)}), bf16[16,8,4096]{2,0,1:T(8,128)(2,1)}) %reduce-scatter.3.cloned.1.call-update) | async-done | bytes 1048592 | tf_op jit(solution)/shard_map/reduce_scatter | solution.py:161
  412.3 2.8 copy.87
  415.1 7.2 %all-to-all-start.1 = ((bf16[16,8,4096]{2,1,0:T(8,128)(2,1)}), bf16[16,8,4096]{2,1,0:T(8,128)(2,1)S(1)}, u32[]{:S(2)}, u32[]{:S(2)}) async-start(bf16[16,8,4096]{2,1,0:T(8,128)(2,1)} %copy.87), calls=%async_computation.2 | async-start | bytes 2097152 | tf_op jit(solution)/shard_map/all_to_all | solution.py:169
  422.5 19.4 %all-to-all-done.1 = bf16[16,8,4096]{2,1,0:T(8,128)(2,1)S(1)} async-done(((bf16[16,8,4096]{2,1,0:T(8,128)(2,1)}), bf16[16,8,4096]{2,1,0:T(8,128)(2,1)S(1)}, u32[]{:S(2)}, u32[]{:S(2)}) %all-to-all-start.1) | async-done | bytes 1048608 | tf_op jit(solution)/shard_map/all_to_all | solution.py:169
  442.1 1.4 fusion.9
  (675 shorter events, 41.7 us)
Async XLA Ops:
  6.5 8.1 %copy-start = (bf16[512,288]{0,1:T(8,128)(2,1)S(1)}, bf16[512,288]{0,1:T(8,128)(2,1)}, u32[]{:S(2)}) copy-start(bf16[512,288]{0,1:T(8,128)(2,1)} %param.27) | copy-start | bytes 884740
  6.5 9.2 %copy-start.3 = (f32[16,512]{1,0:T(8,128)S(1)}, f32[16,512]{1,0:T(8,128)}, u32[]{:S(2)}) copy-start(f32[16,512]{1,0:T(8,128)} %param.30) | copy-start | bytes 98308
  6.5 59.7 %all-gather.7.cloned.1.call-start = ((), (), s32[]{:S(2)}) async-start(), calls=%async_computation.5 | async-start | bytes 3342336 | tf_op jit(solution)/shard_map/all_gather | solution.py:16
  7.3 5.0 %collective-permute-start = (bf16[3,4,512]{2,1,0:T(4,128)(2,1)S(1)}, bf16[3,4,512]{2,1,0:T(4,128)(2,1)S(1)}, u32[]{:S(2)}, u32[]{:S(2)}) collective-permute-start(bf16[3,4,512]{2,1,0:T(4,128)(2,1)S(1)} %slice.38), channel_id=1, source_target_pairs={{0,16},{16,32},{32,48},{48,64},{64,80},{80,96},{96,112},{1,17},{17... | collective-permute-start | bytes 36872 | tf_op jit(solution)/shard_map/ppermute | solution.py:22
  10.1 59.4 %copy-start.2 = (bf16[256,512]{1,0:T(8,128)(2,1)S(1)}, bf16[256,512]{1,0:T(8,128)(2,1)}, u32[]{:S(2)}) copy-start(bf16[256,512]{1,0:T(8,128)(2,1)} %param.28) | copy-start | bytes 786436
  10.1 59.4 %copy-start.6 = (f32[512]{0:T(512)S(1)}, f32[512]{0:T(512)}, u32[]{:S(2)}) copy-start(f32[512]{0:T(512)} %param.29) | copy-start | bytes 6148
  15.6 246.1 %all-reduce.3.cloned.1.call-start = ((), (), s32[]{:S(2)}) async-start(), calls=%async_computation.6 | async-start | bytes 4194304
  70.5 95.6 %copy-start.7 = (f32[512]{0:T(512)S(1)}, f32[512]{0:T(512)}, u32[]{:S(2)}) copy-start(f32[512]{0:T(512)} %param.31) | copy-start | bytes 6148
  167.4 4.9 %copy-start.5 = (s32[4,4,2]{1,2,0:T(2,128)S(1)}, s32[4,4,2]{1,2,0:T(2,128)}, u32[]{:S(2)}) copy-start(s32[4,4,2]{1,2,0:T(2,128)} %param.35) | copy-start | bytes 388
  167.4 5.7 %copy-start.10 = (u32[128]{0:T(128)S(1)}, u32[128]{0:T(128)}, u32[]{:S(2)}) copy-start(u32[128]{0:T(128)} %constant.79) | copy-start | bytes 1540
  167.4 95.3 %copy-start.1 = (bf16[4,4,4096]{2,1,0:T(4,128)(2,1)S(1)}, bf16[4,4,4096]{2,1,0:T(4,128)(2,1)}, u32[]{:S(2)}) copy-start(bf16[4,4,4096]{2,1,0:T(4,128)(2,1)} %param.33) | copy-start | bytes 393220
  167.5 95.6 %copy-start.4 = (f32[4096]{0:T(1024)S(1)}, f32[4096]{0:T(1024)}, u32[]{:S(2)}) copy-start(f32[4096]{0:T(1024)} %param.34) | copy-start | bytes 49156
  172.3 158.9 %all-gather.5.cloned.1.call-start = ((), (), s32[]{:S(2)}) async-start(), calls=%async_computation.3 | async-start | bytes 9437184 | tf_op jit(solution)/shard_map/all_gather | solution.py:155
  284.3 127.9 %reduce-scatter.3.cloned.1.call-start = ((), (), s32[]{:S(2)}) async-start(), calls=%async_computation.4 | async-start | bytes 9437184 | tf_op jit(solution)/shard_map/reduce_scatter | solution.py:161
  331.2 11.1 %copy-start.9 = (bf16[128,8,4096]{2,1,0:T(8,128)(2,1)S(1)}, bf16[128,8,4096]{2,1,0:T(8,128)(2,1)}, u32[]{:S(2)}) copy-start(bf16[128,8,4096]{2,1,0:T(8,128)(2,1)} %all-gather.5.cloned.1.call-done) | copy-start | bytes 25165828
  331.2 21.0 %slice-start = ((s8[6291456]{0:T(1024)(128)(4,1)}), s8[4194304]{0:T(1024)(128)(4,1)S(1)}, s32[]{:S(2)}) async-start(s8[6291456]{0:T(1024)(128)(4,1)} %bitcast.123), calls=%async_computation.7 | async-start | bytes 8388608
  342.3 10.0 %slice-start.1 = ((s8[6291456]{0:T(1024)(128)(4,1)}), s8[2097152]{0:T(1024)(128)(4,1)S(1)}, s32[]{:S(2)}) async-start(s8[6291456]{0:T(1024)(128)(4,1)} %bitcast.123), calls=%async_computation.8 | async-start | bytes 4194304
  361.2 61.1 %copy-start.8 = (bf16[4,4,2]{1,2,0:T(2,128)(2,1)S(1)}, bf16[4,4,2]{1,2,0:T(2,128)(2,1)}, u32[]{:S(2)}) copy-start(bf16[4,4,2]{1,2,0:T(2,128)(2,1)} %param.36) | copy-start | bytes 196
  415.1 26.8 %all-to-all-start.1 = ((bf16[16,8,4096]{2,1,0:T(8,128)(2,1)}), bf16[16,8,4096]{2,1,0:T(8,128)(2,1)S(1)}, u32[]{:S(2)}, u32[]{:S(2)}) async-start(bf16[16,8,4096]{2,1,0:T(8,128)(2,1)} %copy.87), calls=%async_computation.2 | async-start | bytes 2097152 | tf_op jit(solution)/shard_map/all_to_all | solution.py:169
Sparse Core Ops, SparseCore 0:
  15.8 50.4 all-gather.6
  172.4 89.2 all-reduce.2
  284.5 46.7 all-gather.4
  361.3 50.9 reduce-scatter.2
